TPU v7x, 32 devices: a whole 2x2x4 slice. The times are simulated.
32 devices in a mesh: node: 8 (over z, y), local: 4 (over x, core).
Axes of the slice: x: 2, y: 2, z: 4, core: 2. Of those that a mesh axis runs over, the one named last changes fastest.
Arguments:
- inputs: bfloat16 [64, 3584], P('node', 'local'), may hold values from -6 to 6
- out_grad: bfloat16 [64, 3584], P('node', 'local'), may hold values from -6 to 6
- expert_ids: int32 [64, 2], replicated, may hold values from 0 to 7, all different within a row; in each aligned block of 64 rows (0 to 63, 64 to 127, ...) at most 32 rows name the same one
- route_probs: float32 [64, 2], replicated, may hold values from 0.1 to 1
- gate_weight: bfloat16 [8, 3584, 1024], P('node', None, 'local'), may hold values from -0.09375 to 0.09375
- up_weight: bfloat16 [8, 3584, 1024], P('node', None, 'local'), may hold values from -0.09375 to 0.09375
- down_weight: bfloat16 [8, 1024, 3584], P('node', 'local'), may hold values from -0.1875 to 0.1875
Outputs:
- d_inputs: bfloat16 [64, 3584], P('node', 'local')
Inputs may be any that keep to these rules, and one draw needn't show every extreme that they name: `expert_ids`: each row names 2 different experts. No expert is named by more than 32 pairs in all, a bound that some block reaches.
All inputs are finite; a program needn't handle non-finite values.
Results may differ from a plain program's by a relative error of at most 0.0064.
Values may be sent and summed in bfloat16 or wider, within the bound.
No kernel may reach another device: no remote copies, remote signals or barrier semaphores. Data moves between devices by JAX's collectives and lax.ppermute only.
A program may use at most 64 MiB of HBM per device.

v0:
```python
import jax
import jax.numpy as jnp
from jax import lax
from jax.sharding import PartitionSpec as P


def slot_tables(expert_ids, route_probs, expert, cape):
    flat = expert_ids.reshape(-1)
    hit = (flat == expert).astype(jnp.int32)
    rank = jnp.cumsum(hit) - 1
    slots = jnp.arange(cape, dtype=jnp.int32)
    onehot = jnp.where((rank[None, :] == slots[:, None]) & (hit[None, :] == 1), 1.0, 0.0).astype(
        jnp.float32
    )
    onehot = onehot.reshape(cape, expert_ids.shape[0], expert_ids.shape[1])
    select = jnp.sum(onehot, axis=2)
    scale = jnp.sum(onehot * route_probs[None, :, :], axis=(1, 2))
    return (select, scale)


def expert_terms(x_rows, g_rows, gate_w, up_w, down_w):
    gate = jnp.dot(x_rows, gate_w, preferred_element_type=jnp.float32)
    up = jnp.dot(x_rows, up_w, preferred_element_type=jnp.float32)
    sig = jax.nn.sigmoid(gate)
    act = gate * sig
    d_hidden = lax.dot_general(
        g_rows, down_w, (((1,), (1,)), ((), ())), preferred_element_type=jnp.float32
    )
    d_up = (d_hidden * act).astype(jnp.bfloat16)
    d_gate = (d_hidden * up * sig * (1.0 + gate * (1.0 - sig))).astype(jnp.bfloat16)
    first = lax.dot_general(
        d_gate, gate_w, (((1,), (1,)), ((), ())), preferred_element_type=jnp.float32
    )
    second = lax.dot_general(
        d_up, up_w, (((1,), (1,)), ((), ())), preferred_element_type=jnp.float32
    )
    return first + second


def shards(inputs, out_grad, expert_ids, route_probs, gate_weight, up_weight, down_weight):
    expert = lax.axis_index("node")
    tok_rows = inputs.shape[0]
    width = inputs.shape[1]
    cape = 2 * tok_rows * expert_ids.shape[1]
    select, scale = slot_tables(expert_ids, route_probs, expert, cape)
    sel_half = select.astype(jnp.bfloat16)
    every_x, every_g = (
        lax.all_gather(inputs, "node", axis=0, tiled=True),
        lax.all_gather(out_grad, "node", axis=0, tiled=True),
    )
    x_sum = jnp.dot(sel_half, every_x, preferred_element_type=jnp.float32)
    g_sum = jnp.dot(sel_half, every_g, preferred_element_type=jnp.float32)
    x_part = x_sum.astype(jnp.bfloat16)
    g_part = (scale[:, None] * g_sum).astype(jnp.bfloat16)
    x_rows, g_rows = (
        lax.all_gather(x_part, "local", axis=1, tiled=True),
        lax.all_gather(g_part, "local", axis=1, tiled=True),
    )
    partial_value = expert_terms(x_rows, g_rows, gate_weight[0], up_weight[0], down_weight[0])
    summed = lax.psum(partial_value, "local")
    mine = lax.dynamic_slice_in_dim(summed, lax.axis_index("local") * width, width, 1)
    d_rows = mine.astype(jnp.bfloat16)
    return lax.psum_scatter(
        lax.dot_general(
            sel_half, d_rows, (((0,), (0,)), ((), ())), preferred_element_type=jnp.float32
        ),
        "node",
        scatter_dimension=0,
        tiled=True,
    ).astype(jnp.bfloat16)


def solution(mesh):
    placed = (
        P("node", "local"),
        P("node", "local"),
        P(),
        P(),
        P("node", None, "local"),
        P("node", None, "local"),
        P("node", "local", None),
    )
    return jax.shard_map(
        shards, mesh=mesh, in_specs=placed, out_specs=P("node", "local"), check_vma=False
    )
```

profile of v0, /device:TPU:0, one launch (start us, length us, event | category | flops | bytes accessed | tf_op | source)
XLA Modules:
  0.0 141.6 jit_solution(6451418618623909036)
XLA Ops:
  0.0 0.0 copy-start
  0.0 0.0 copy-start.2
  0.0 0.8 broadcast_compare_fusion
  0.8 0.1 copy.17
  0.9 0.1 reshape.51
  1.1 0.3 reduce-window_clone.1
  1.4 0.1 sub.10
  1.5 0.1 copy.18
  1.6 0.0 copy-start.1
  1.6 1.0 select_reduce_fusion
  2.6 32.6 %all_gather.12 = bf16[64,896]{1,0:T(8,128)(2,1)S(1)} all-gather(bf16[8,896]{1,0:T(8,128)(2,1)} %param.8), channel_id=1, replica_groups=mesh['node'=8,'local'=4] {'node'}, dimensions={0}, use_global_device_ids=true | all-gather | bytes 129024 | tf_op jit(solution)/shard_map/all_gather | solution.py:49
  35.2 0.1 fusion.9
  35.3 5.7 %all_gather.13 = bf16[32,3584]{1,0:T(8,128)(2,1)S(1)} all-gather(bf16[32,896]{1,0:T(8,128)(2,1)S(1)} %fusion.9), channel_id=1, replica_groups=mesh['node'=8,'local'=4] {'local'}, dimensions={1}, use_global_device_ids=true | all-gather | bytes 286720 | tf_op jit(solution)/shard_map/all_gather | solution.py:57
  41.0 2.1 %fusion.7 = f32[32,256]{1,0:T(8,128)S(1)} fusion(bf16[32,3584]{1,0:T(8,128)(2,1)S(1)} %all_gather.13, bf16[1,256,3584]{2,1,0:T(8,128)(2,1)} %param.13), kind=kOutput, calls=%fused_computation.8 | convolution fusion | flops 58720256 | bytes 2097152 | tf_op jit(solution)/shard_map/dot_general | solution.py:26
  43.1 0.0 copy-done.2
  43.2 30.6 %all_gather.14 = bf16[64,896]{1,0:T(8,128)(2,1)S(1)} all-gather(bf16[8,896]{1,0:T(8,128)(2,1)S(1)} %copy-done.2), channel_id=1, replica_groups=mesh['node'=8,'local'=4] {'node'}, dimensions={0}, use_global_device_ids=true | all-gather | bytes 129024 | tf_op jit(solution)/shard_map/all_gather | solution.py:48
  73.7 0.1 convolution_convert_fusion
  73.9 5.7 %all_gather.15 = bf16[32,3584]{1,0:T(8,128)(2,1)S(1)} all-gather(bf16[32,896]{1,0:T(8,128)(2,1)S(1)} %convolution_convert_fusion), channel_id=1, replica_groups=mesh['node'=8,'local'=4] {'local'}, dimensions={1}, use_global_device_ids=true | all-gather | bytes 286720 | tf_op jit(solution)/shard_map/all_gather | solution.py:56
  79.6 0.0 copy-done.1
  79.6 0.4 fusion.2
  80.0 0.0 copy-done
  80.0 2.8 %fusion = f32[32,3584]{1,0:T(8,128)S(1)} fusion(bf16[1,3584,256]{2,1,0:T(8,128)(2,1)} %param.11, f32[32,256]{1,0:T(8,128)S(1)} %fusion.7, bf16[32,3584]{1,0:T(8,128)(2,1)S(1)} %all_gather.15, bf16[1,3584,256]{2,1,0:T(8,128)(2,1)S(1)} %copy-done, f32[32,256]{1,0:T(8,128)S(1)} %fusion.2), kind=kOutput, calls=%fused_computation.1 | convolution fusion | flops 117522432 | bytes 4423680 | tf_op jit(solution)/shard_map/dot_general | solution.py:31
  82.8 0.0 copy-start.3
  82.8 0.7 convolution_add_fusion
  83.5 16.3 %all-reduce.3 = bf16[32,3584]{1,0:T(8,128)(2,1)S(1)} all-reduce(f32[32,3584]{1,0:T(8,128)S(1)} %convolution_add_fusion), channel_id=1, replica_groups=mesh['node'=8,'local'=4] {'local'}, use_global_device_ids=true, to_apply=%region_3.4 | all-reduce | flops 114688 | bytes 688128 | tf_op jit(solution)/shard_map/psum | solution.py:60
  99.8 0.2 fusion.24
  100.0 39.7 %all-reduce.4 = bf16[64,896]{1,0:T(8,128)(2,1)S(1)} all-reduce(f32[64,896]{1,0:T(8,128)S(1)} %fusion.24), channel_id=2, replica_groups=mesh['node'=8,'local'=4] {'node'}, use_global_device_ids=true, to_apply=%region_4.5.clone | all-reduce | flops 57344 | bytes 344064
  139.7 0.0 copy-done.3
  139.8 0.6 dynamic-slice
  141.0 0.6 dynamic-slice_convert_fusion.2
  (1 shorter events, 0.0 us)
Async XLA Ops:
  0.0 80.0 %copy-start = (bf16[1,3584,256]{2,1,0:T(8,128)(2,1)S(1)}, bf16[1,3584,256]{2,1,0:T(8,128)(2,1)}, u32[]{:S(2)}) copy-start(bf16[1,3584,256]{2,1,0:T(8,128)(2,1)} %param.12) | copy-start | bytes 5505028
  0.0 43.1 %copy-start.2 = (bf16[8,896]{1,0:T(8,128)(2,1)S(1)}, bf16[8,896]{1,0:T(8,128)(2,1)}, u32[]{:S(2)}) copy-start(bf16[8,896]{1,0:T(8,128)(2,1)} %param.7) | copy-start | bytes 43012
  1.6 78.0 %copy-start.1 = (bf16[1,3584,256]{2,1,0:T(8,128)(2,1)S(1)}, bf16[1,3584,256]{2,1,0:T(8,128)(2,1)}, u32[]{:S(2)}) copy-start(bf16[1,3584,256]{2,1,0:T(8,128)(2,1)} %param.11) | copy-start | bytes 5505028
  82.8 56.9 %copy-start.3 = (u32[32]{0:T(128)S(1)}, u32[32]{0:T(128)}, u32[]{:S(2)}) copy-start(u32[32]{0:T(128)} %constant.33) | copy-start | bytes 388
where the time goes:
time: 142 us
  blocking collectives  131 us (92%)
  matrix products  6.46 us (5%)
  other arithmetic  2.11 us (1%)
  local copies, waits for them, and re-layouts  1.68 us (1%)
    unnamed x1, blocking collectives  39.7 us
    all_gather x1, blocking collectives, shards(): lax.all_gather(out_grad, 'node', axis=0, tiled=True)  32.6 us
    all_gather x1, blocking collectives, shards(): lax.all_gather(inputs, 'node', axis=0, tiled=True)  30.6 us
    psum x1, blocking collectives, shards(): summed = lax.psum(partial_value, 'local')  16.3 us
    all_gather x1, blocking collectives, shards(): lax.all_gather(g_part, 'local', axis=1, tiled=True)  5.69 us
    all_gather x1, blocking collectives, shards(): lax.all_gather(x_part, 'local', axis=1, tiled=True)  5.69 us

commit v1 on v0

--- a/solution.py
+++ b/solution.py
@@ -57,7 +57,7 @@
         lax.all_gather(g_part, "local", axis=1, tiled=True),
     )
     partial_value = expert_terms(x_rows, g_rows, gate_weight[0], up_weight[0], down_weight[0])
-    summed = lax.psum(partial_value, "local")
+    summed = jnp.sum(lax.all_gather(partial_value, "local"), axis=0)
     mine = lax.dynamic_slice_in_dim(summed, lax.axis_index("local") * width, width, 1)
     d_rows = mine.astype(jnp.bfloat16)
     return lax.psum_scatter(

time: 142 us -> 163 us (1.15)
  waiting for transfers between devices: 0 us -> 20.9 us
  blocking collectives: 131 us -> 115 us
  between operations: 0.74 us -> 14.1 us
    all_gather x0 -> x1, waiting for transfers between devices: none -> 20.9 us  [shards(): summed = jnp.sum(lax.all_gather(partial_value, 'local'), axis=0)]
    psum x1 -> x0, blocking collectives: 16.3 us -> none  [shards(): summed = lax.psum(partial_value, 'local')]
    reduce_sum x0 -> x1, other arithmetic: none -> 1.63 us  [shards(): summed = jnp.sum(lax.all_gather(partial_value, 'local'), axis=0)]
  transfers between devices with their start and end apart: 0 -> 1, of which waited for: 0 -> 1; matrix products, arithmetic and copies ran while one was open for 0% -> 0% of each run, Pallas kernels for 0% -> 0%
where the time goes in v1:
time: 163 us; the launch traced here: 162 us
  blocking collectives  115 us (71%)
  waiting for transfers between devices  20.9 us (13%)
  between operations  14.1 us (9%)
  matrix products  7.26 us (4%)
  other arithmetic  3.58 us (2%)
  local copies, waits for them, and re-layouts  1.68 us (1%)
    unnamed x1, blocking collectives  39.9 us
    all_gather x1, blocking collectives, shards(): lax.all_gather(out_grad, 'node', axis=0, tiled=True)  32.8 us
    all_gather x1, blocking collectives, shards(): lax.all_gather(inputs, 'node', axis=0, tiled=True)  30.8 us
    all_gather x1, waiting for transfers between devices, shards(): summed = jnp.sum(lax.all_gather(partial_value, 'local'), axis=0)  20.9 us
    all_gather x1, blocking collectives, shards(): lax.all_gather(g_part, 'local', axis=1, tiled=True)  5.69 us
    all_gather x1, blocking collectives, shards(): lax.all_gather(x_part, 'local', axis=1, tiled=True)  5.69 us
  transfers between devices with their start and end apart: 1, of which 1 were waited for; matrix products, arithmetic and copies ran while one was open for 0% of the time, Pallas kernels for 0%

profile of v1, /device:TPU:0, one launch (start us, length us, event | category | flops | bytes accessed | tf_op | source)
XLA Modules:
  0.0 162.3 jit_solution(952884830850161775)
XLA Ops:
  6.5 0.0 copy-start
  6.5 0.0 all-gather.3.cloned.1.call-start
  6.5 0.8 broadcast_compare_fusion
  7.4 0.1 copy.17
  7.5 0.1 reshape.51
  7.6 0.3 reduce-window_clone.1
  7.9 0.1 sub.10
  8.1 0.1 copy.18
  8.1 0.0 copy-start.1
  8.1 32.8 %all_gather.18 = bf16[64,896]{1,0:T(8,128)(2,1)S(1)} all-gather(bf16[8,896]{1,0:T(8,128)(2,1)} %param.8), channel_id=1, replica_groups=mesh['node'=8,'local'=4] {'node'}, dimensions={0}, use_global_device_ids=true | all-gather | bytes 129024 | tf_op jit(solution)/shard_map/all_gather | solution.py:49
  40.9 0.8 select_reduce_fusion
  41.7 0.1 fusion.9
  41.8 5.7 %all_gather.19 = bf16[32,3584]{1,0:T(8,128)(2,1)S(1)} all-gather(bf16[32,896]{1,0:T(8,128)(2,1)S(1)} %fusion.9), channel_id=1, replica_groups=mesh['node'=8,'local'=4] {'local'}, dimensions={1}, use_global_device_ids=true | all-gather | bytes 286720 | tf_op jit(solution)/shard_map/all_gather | solution.py:57
  47.5 30.8 %all_gather.20 = bf16[64,896]{1,0:T(8,128)(2,1)S(1)} all-gather(bf16[8,896]{1,0:T(8,128)(2,1)} %param.7), channel_id=1, replica_groups=mesh['node'=8,'local'=4] {'node'}, dimensions={0}, use_global_device_ids=true | all-gather | bytes 129024 | tf_op jit(solution)/shard_map/all_gather | solution.py:48
  78.3 0.1 convolution_convert_fusion
  78.5 5.7 %all_gather.21 = bf16[32,3584]{1,0:T(8,128)(2,1)S(1)} all-gather(bf16[32,896]{1,0:T(8,128)(2,1)S(1)} %convolution_convert_fusion), channel_id=1, replica_groups=mesh['node'=8,'local'=4] {'local'}, dimensions={1}, use_global_device_ids=true | all-gather | bytes 286720 | tf_op jit(solution)/shard_map/all_gather | solution.py:56
  84.2 2.1 %fusion.7 = f32[32,256]{1,0:T(8,128)S(1)} fusion(bf16[32,3584]{1,0:T(8,128)(2,1)S(1)} %all_gather.19, bf16[1,256,3584]{2,1,0:T(8,128)(2,1)} %param.13), kind=kOutput, calls=%fused_computation.8 | convolution fusion | flops 58720256 | bytes 2097152 | tf_op jit(solution)/shard_map/dot_general | solution.py:26
  86.3 0.0 copy-done.1
  86.3 0.4 fusion.2
  86.7 0.0 copy-done
  86.7 2.8 %fusion = f32[32,3584]{1,0:T(8,128)S(1)} fusion(bf16[1,3584,256]{2,1,0:T(8,128)(2,1)} %param.11, f32[32,256]{1,0:T(8,128)S(1)} %fusion.7, bf16[32,3584]{1,0:T(8,128)(2,1)S(1)} %all_gather.21, bf16[1,3584,256]{2,1,0:T(8,128)(2,1)S(1)} %copy-done, f32[32,256]{1,0:T(8,128)S(1)} %fusion.2), kind=kOutput, calls=%fused_computation.1 | convolution fusion | flops 117522432 | bytes 4423680 | tf_op jit(solution)/shard_map/dot_general | solution.py:31
  89.6 0.0 copy-start.2
  89.6 1.4 convolution_add_fusion
  91.0 0.0 all-gather.3.cloned.1.call-update
  91.0 0.0 copy-done.2
  91.0 0.6 dynamic-slice
  92.3 20.9 %all-gather.3.cloned.1.call-done = f32[128,3584]{1,0:T(8,128)} async-done(((f32[32,3584]{1,0:T(8,128)}), f32[128,3584]{1,0:T(8,128)}) %all-gather.3.cloned.1.call-update) | async-done | bytes 1835024 | tf_op jit(solution)/shard_map/all_gather | solution.py:60
  113.1 1.6 %reduce_sum.29 = bf16[32,3584]{1,0:T(8,128)(2,1)S(1)} reduce(f32[4,32,3584]{2,1,0:T(8,128)} %bitcast.33, f32[]{:T(128)} %constant.24.clone.1), dimensions={0}, to_apply=%region_3.4 | reduce | flops 344064 | bytes 2064388 | tf_op jit(solution)/shard_map/reduce_sum | solution.py:60
  114.8 0.2 fusion.24
  115.0 39.9 %all-reduce.2 = bf16[64,896]{1,0:T(8,128)(2,1)S(1)} all-reduce(f32[64,896]{1,0:T(8,128)S(1)} %fusion.24), channel_id=3, replica_groups=mesh['node'=8,'local'=4] {'node'}, use_global_device_ids=true, to_apply=%region_4.5.clone | all-reduce | flops 57344 | bytes 344064
  154.9 0.6 dynamic-slice_convert_fusion.2
  (1 shorter events, 0.0 us)
Async XLA Ops:
  6.5 80.2 %copy-start = (bf16[1,3584,256]{2,1,0:T(8,128)(2,1)S(1)}, bf16[1,3584,256]{2,1,0:T(8,128)(2,1)}, u32[]{:S(2)}) copy-start(bf16[1,3584,256]{2,1,0:T(8,128)(2,1)} %param.12) | copy-start | bytes 5505028
  6.5 106.6 %all-gather.3.cloned.1.call-start = ((), (), s32[]{:S(2)}) async-start(), calls=%async_computation | async-start | bytes 2293760 | tf_op jit(solution)/shard_map/all_gather | solution.py:60
  8.1 78.1 %copy-start.1 = (bf16[1,3584,256]{2,1,0:T(8,128)(2,1)S(1)}, bf16[1,3584,256]{2,1,0:T(8,128)(2,1)}, u32[]{:S(2)}) copy-start(bf16[1,3584,256]{2,1,0:T(8,128)(2,1)} %param.11) | copy-start | bytes 5505028
  89.6 1.5 copy-start.2
Sparse Core Ops, SparseCore 0:
  91.1 21.9 all-gather.2
